TPU v7x, 512 devices: a whole 4x8x8 slice. The times are simulated.
512 devices in a mesh: feat: 128 (over x, y, z_hi), rows: 4 (over z_lo, core).
Axes of the slice: x: 4, y: 8, z: 8 (z_hi: 4, z_lo: 2; z = z_hi * 2 + z_lo), core: 2. Of those that a mesh axis runs over, the one named last changes fastest.
Arguments:
- binned: int32 [8192, 8192], P('rows', 'feat'), may hold values from 0 to 255
- node_of: int32 [8192], P('rows'), may hold values from 0 to 31
- margin: float32 [8192], P('rows'), may hold values from -6 to 6
- labels: float32 [8192], P('rows'), may hold values from 0 to 1
- split_feature: int32 [32], replicated, may hold values from 0 to 8191
- split_bin: int32 [32], replicated, may hold values from 0 to 255
Outputs:
- histogram: float32 [32, 2, 8192, 256], P('rows', None, 'feat')
- margin_out: float32 [8192], P('rows')
- child_out: int32 [8192], P('rows')
- grad_out: float32 [2, 8192], P(None, 'rows')
All inputs are finite; a program needn't handle non-finite values.
Results may differ from a plain program's by a relative error of at most 0.0045.
Values may be sent and summed in bfloat16 or wider, within the bound.
No kernel may reach another device: no remote copies, remote signals or barrier semaphores. Data moves between devices by JAX's collectives and lax.ppermute only.
A program may use at most 64 MiB of HBM per device.

v0:
```python
import jax
import jax.numpy as jnp
from jax import lax
from jax.sharding import PartitionSpec as P

BINS = 256


def leaf_table(selected, split_rows):
    below = (jnp.arange(selected.shape[2])[None, :] <= split_rows[:, None]).astype(jnp.float32)
    left = jnp.sum(selected * below[:, None, :], axis=2)
    whole = jnp.sum(selected, axis=2)
    return jnp.concatenate([left, whole], axis=1)


def node_sums(nodes_here, feature_ids, split_rows, feat_start):
    feat_count = nodes_here.shape[2]
    local = feature_ids - feat_start
    owned = (local >= 0) & (local < feat_count)
    chooser = ((local[:, None] == jnp.arange(feat_count)[None, :]) & owned[:, None]).astype(
        jnp.float32
    )
    selected = jnp.einsum("ncfb,nf->ncb", nodes_here, chooser, precision=lax.Precision.HIGHEST)
    return leaf_table(selected, split_rows)


def on_device(binned, node_of, margin, labels, split_feature, split_bin):
    row_count, feat_count = binned.shape
    node_total = split_feature.shape[0]
    feat_start = lax.axis_index("feat") * feat_count
    probability = jax.nn.sigmoid(margin)
    gradient = (probability - labels).astype(jnp.bfloat16)
    hessian = (probability * (1.0 - probability)).astype(jnp.bfloat16)
    node_hot = node_of[:, None] == jnp.arange(node_total, dtype=jnp.int32)[None, :]
    hot_float = node_hot.astype(jnp.bfloat16)
    weights = jnp.stack([gradient[:, None] * hot_float, hessian[:, None] * hot_float], axis=2)
    weights = weights.reshape(row_count, 2 * node_total)
    row_feature = jnp.sum(jnp.where(node_hot, split_feature[None, :], 0), axis=1)
    row_cut = jnp.sum(jnp.where(node_hot, split_bin[None, :], 0), axis=1)
    local = row_feature - feat_start
    owned = (local >= 0) & (local < feat_count)
    column_hot = jnp.arange(feat_count, dtype=jnp.int32)[None, :] == local[:, None]
    row_value = jnp.sum(jnp.where(column_hot, binned, 0), axis=1)
    right_bits = ((row_value > row_cut) & owned).astype(jnp.int32)
    go_right = lax.psum(right_bits, "feat")
    bin_ids = jnp.arange(BINS, dtype=jnp.int32)
    group = 8

    def add_block(block_index, partial_value):
        columns = lax.dynamic_slice_in_dim(binned, block_index * group, group, 1)
        one_hot = (columns.T[:, :, None] == bin_ids[None, None, :]).astype(jnp.bfloat16)
        piece = jnp.einsum("rk,frb->kfb", weights, one_hot, preferred_element_type=jnp.float32)
        return lax.dynamic_update_slice_in_dim(partial_value, piece, block_index * group, 1)

    partial_value = lax.fori_loop(
        0,
        feat_count // group,
        add_block,
        jnp.zeros((2 * node_total, feat_count, BINS), jnp.float32),
    )
    partial_value = partial_value.reshape(node_total, 2, feat_count, BINS).astype(jnp.bfloat16)
    node_share = node_total // lax.axis_size("rows")
    node_start = lax.axis_index("rows") * node_share
    summed = lax.psum(partial_value, "rows").astype(jnp.float32)
    histogram = lax.dynamic_slice_in_dim(summed, node_start, node_share, 0)
    table_part = node_sums(summed, split_feature, split_bin, feat_start)
    table = lax.psum(table_part, "feat")
    leaf_left = -table[:, 0] / (table[:, 1] + 1.0)
    leaf_right = -(table[:, 2] - table[:, 0]) / (table[:, 3] - table[:, 1] + 1.0)
    row_left = jnp.sum(jnp.where(node_hot, leaf_left[None, :], 0.0), axis=1)
    row_right = jnp.sum(jnp.where(node_hot, leaf_right[None, :], 0.0), axis=1)
    margin_out = margin + jnp.where(go_right == 1, row_right, row_left)
    child_out = 2 * node_of + go_right
    fresh = jax.nn.sigmoid(margin_out)
    grad_out = jnp.stack([fresh - labels, fresh * (1.0 - fresh)], axis=0)
    return (histogram, margin_out, child_out, grad_out)


def solution(mesh):
    in_specs = (P("rows", "feat"), P("rows"), P("rows"), P("rows"), P(), P())
    out_specs = (P("rows", None, "feat", None), P("rows"), P("rows"), P(None, "rows"))
    return jax.shard_map(
        on_device, mesh=mesh, in_specs=in_specs, out_specs=out_specs, check_vma=False
    )
```

profile of v0, /device:TPU:64, one launch (start us, length us, event | category | flops | bytes accessed | tf_op | source)
XLA Modules:
  0.0 510.7 jit_solution(691972997853340159)
XLA Ops:
  7.2 0.0 copy-start
  7.2 0.0 all-reduce.2.cloned.1.call-start
  7.2 0.8 subtract_convert_fusion
  8.0 1.1 compare_select_fusion.1
  9.1 0.6 pad_maximum_fusion
  9.7 0.1 reshape.186
  9.8 0.2 broadcast_in_dim.65
  10.1 0.0 copy-done
  10.1 35.7 %while.14 = (s32[]{:T(128)}, bf16[64,64,256]{2,0,1:T(8,128)(2,1)S(1)}, s32[2048,64]{0,1:T(8,128)S(1)}, bf16[2048,64]{0,1:T(8,128)(2,1)S(1)}, s32[]{:T(128)}, /*index=5*/s32[]{:T(128)}, s32[]{:T(128)}, s32[]{:T(128)}) while((s32[]{:T(128)}, bf16[64,64,256]{2,0,1:T(8,128)(2,1)S(1)}, s32[2048,64]{0,1:T(8,128)S(1)}, ...), condition=%wide.region_1.2_spmd.clone, body=%wide.region_0.1_spmd.clone.sunk | while | flops 541065216 | bytes 983187 | solution.py:55
  10.1 4.4 fusion.21
  14.6 4.4 fusion.21
  19.1 4.4 fusion.21
  23.5 4.4 fusion.21
  28.0 4.4 fusion.21
  32.5 4.4 fusion.21
  36.9 4.4 fusion.21
  41.4 4.4 fusion.21
  45.8 2.5 copy.11
  48.3 0.0 copy-start.1
  48.3 0.0 copy-start.5
  48.3 0.0 copy-start.6
  48.3 0.0 copy-start.2
  48.3 0.0 copy-start.3
  48.3 0.0 all-reduce.2.cloned.1.call-update
  48.3 0.6 copy-done.1
  49.0 0.0 copy-done.5
  49.0 0.0 copy-done.6
  49.0 0.2 select_reduce_fusion.3
  49.2 0.1 select_reduce_fusion
  49.3 34.9 %psum.22 = s32[2048]{0:T(1024)S(1)} all-reduce(s32[2048]{0:T(1024)S(1)} %and_convert_fusion), channel_id=1, replica_groups=mesh['feat'=128,'rows'=4] {'feat'}, use_global_device_ids=true, to_apply=%region_6.7 | all-reduce | flops 2048 | bytes 16384 | tf_op jit(solution)/shard_map/psum | solution.py:45
  84.1 0.1 fusion.12
  84.2 0.6 multiply_add_fusion
  84.8 0.1 fusion.10
  84.9 33.3 %all-reduce.2.cloned.1.call-done = bf16[32,2,64,256]{3,2,1,0:T(8,128)(2,1)} async-done(((bf16[32,2,64,256]{3,2,1,0:T(8,128)(2,1)}), bf16[32,2,64,256]{3,2,1,0:T(8,128)(2,1)}) %all-reduce.2.cloned.1.call-update) | async-done | bytes 2097168 | tf_op jit(solution)/shard_map/psum | solution.py:64
  118.2 2.0 fusion.8
  120.2 0.1 fusion.7
  120.3 380.5 %psum.23 = f32[32,4]{0,1:T(4,128)S(1)} all-reduce(f32[32,4]{0,1:T(4,128)S(1)} %pad_maximum_fusion.2), channel_id=1, replica_groups=mesh['feat'=128,'rows'=4] {'feat'}, use_global_device_ids=true, to_apply=%region_9.10 | all-reduce | flops 128 | bytes 1024 | tf_op jit(solution)/shard_map/psum | solution.py:67
  500.8 0.2 select_reduce_fusion.1
  501.0 0.0 copy-done.2
  501.0 0.0 copy-done.3
  501.0 0.0 copy-start.4
  501.1 0.6 pad_maximum_fusion.1
  501.7 2.1 dynamic-slice_convert_fusion
  503.8 0.0 copy-done.4
  (15 shorter events, 0.2 us)
Async XLA Ops:
  7.2 2.9 copy-start
  7.2 111.0 %all-reduce.2.cloned.1.call-start = ((), (), s32[]{:S(2)}) async-start(), calls=%async_computation | async-start | bytes 4194304 | tf_op jit(solution)/shard_map/psum | solution.py:64
  48.3 0.7 copy-start.1
  48.3 0.7 copy-start.5
  48.3 0.7 copy-start.6
  48.3 452.7 %copy-start.2 = (f32[2048]{0:T(1024)S(1)}, f32[2048]{0:T(1024)}, u32[]{:S(2)}) copy-start(f32[2048]{0:T(1024)} %param.11) | copy-start | bytes 24580
  48.3 452.7 %copy-start.3 = (f32[2048]{0:T(1024)S(1)}, f32[2048]{0:T(1024)}, u32[]{:S(2)}) copy-start(f32[2048]{0:T(1024)} %param.10) | copy-start | bytes 24580
  501.0 2.8 copy-start.4
Sparse Core Ops, SparseCore 0:
  48.5 69.6 all-reduce.1
where the time goes:
time: 511 us
  blocking collectives  415 us (81%)
  matrix products  37.3 us (7%)
  waiting for transfers between devices  33.3 us (7%)
  between operations  14.2 us (3%)
  other arithmetic  6.54 us (1%)
    psum x1, blocking collectives, on_device(): table = lax.psum(table_part, 'feat')  381 us
    dot_general x8, matrix products, add_block(): jnp.einsum('rk,frb->kfb', weights, one_hot, preferred_element_type=jnp.fl...  35.3 us
    psum x1, blocking collectives, on_device(): go_right = lax.psum(right_bits, 'feat')  34.9 us
    psum x1, waiting for transfers between devices, on_device(): summed = lax.psum(partial_value, 'rows').astype(jnp.float32)  33.3 us
  transfers between devices with their start and end apart: 1, of which 1 were waited for; matrix products, arithmetic and copies ran while one was open for 0% of the time, Pallas kernels for 0%

commit v1 on v0

v1 whole, which is shorter than its diff:
```python
import jax
import jax.numpy as jnp
from jax import lax
from jax.experimental import pallas as pl
from jax.experimental.pallas import tpu as pltpu
from jax.sharding import Mesh
from jax.sharding import PartitionSpec as P

BINS = 256
NODES = 32
ROWS = 2048
FEATS = 64
TILE = 256
FEAT_AXES = ("x", "y", "zh")
ROW_AXES = ("zl", "core")
PLANE = ("x", "y")
LINE = ("zh", "zl", "core")
F32 = jnp.float32
BF16 = jnp.bfloat16
VMEM = pl.BlockSpec(memory_space=pltpu.VMEM)


def iota(shape, dim):
    return lax.broadcasted_iota(jnp.int32, shape, dim)


def cost(flops, moved):
    return pl.CostEstimate(flops=flops, bytes_accessed=moved, transcendentals=0)


def contract_last(a, b):
    return lax.dot_general(a, b, (((1,), (1,)), ((), ())), preferred_element_type=F32)


def bin_hot(row, bins):
    col = jnp.broadcast_to(row, (16, TILE)).astype(BF16)
    col = jnp.concatenate([col] * (BINS // 16), axis=0)
    return jnp.where(bins == col, BF16(1), BF16(0))


def bin_sums(weights_ref, row_of, bins):
    total = None
    for k in range(ROWS // TILE):
        piece = contract_last(weights_ref[:, k * TILE : (k + 1) * TILE], bin_hot(row_of(k), bins))
        total = piece if total is None else total + piece
    return total


def bins_tile():
    return iota((BINS, TILE), 0).astype(F32).astype(BF16)


def stage_kernel(binned, node, margin, labels, feature, cut, weights, columns, pay, chosen):
    here = lax.axis_index("zl") * 2 + lax.axis_index("core")
    feat_start = (
        (lax.axis_index("x") * 8 + lax.axis_index("y")) * 4 + lax.axis_index("zh")
    ) * FEATS
    probability = jax.nn.sigmoid(margin[...])
    gradient = probability - labels[...]
    hessian = probability * (1.0 - probability)
    q = iota((2 * NODES, 1), 0)
    block = q // 16
    block = jnp.where(block < 2, 2 * block + 1, 2 * block - 4)
    node_q = (block * 8 + (q % 16) // 2) ^ (here * 8)
    channel = q % 2
    values = jnp.where(channel == 0, gradient, hessian)
    weights[...] = jnp.where(node[...] == node_q, values, 0.0).astype(BF16)
    local = feature[...] - feat_start
    diagonal = iota((NODES, NODES), 0) == iota((NODES, NODES), 1)
    local_n = jnp.sum(jnp.where(diagonal, local, 0), axis=1, keepdims=True)
    cut_n = jnp.sum(jnp.where(diagonal, cut[...], 0), axis=1, keepdims=True)
    owned_n = (local_n >= 0) & (local_n < FEATS)
    picker = jnp.where(
        iota((FEATS, FEATS), 0) == iota((FEATS, FEATS), 1), 1.0, 0.0
    ).astype(BF16)
    chooser = jnp.where(iota((NODES, FEATS), 1) == local_n, 1.0, 0.0).astype(BF16)
    table_bf = binned[...].astype(F32).astype(BF16)
    columns[...] = contract_last(picker, table_bf)
    split_values = contract_last(chooser, table_bf)
    hot = node[...] == iota((NODES, ROWS), 0)
    value = jnp.sum(jnp.where(hot, split_values, 0.0), axis=0, keepdims=True)
    owned = jnp.sum(jnp.where(hot & owned_n, 1.0, 0.0), axis=0, keepdims=True)
    row_cut = jnp.sum(jnp.where(hot, cut_n.astype(F32), 0.0), axis=0, keepdims=True)
    right = jnp.where(value > row_cut, owned, 0.0)
    chosen[...] = jnp.where(owned > 0.5, value, -1.0)
    bins = bins_tile()
    sums = bin_sums(weights, lambda k: chosen[:, k * TILE : (k + 1) * TILE], bins)
    sums = sums.astype(BF16).astype(F32)
    cut_q = jnp.sum(
        jnp.where(iota((2 * NODES, NODES), 1) == node_q, cut[...], 0), axis=1, keepdims=True
    )
    below = iota((2 * NODES, BINS), 1) <= cut_q
    left = jnp.sum(jnp.where(below, sums, 0.0), axis=1, keepdims=True)
    whole = jnp.sum(sums, axis=1, keepdims=True)
    lane = iota((2 * NODES, 128), 1)
    slot = 2 * node_q + channel
    entries = jnp.where(lane == slot, left, 0.0) + jnp.where(lane == slot + 64, whole, 0.0)
    pay[...] = jnp.zeros((16, 128), F32)
    pay[8:9, :] = jnp.sum(entries, axis=0, keepdims=True)
    half = ROWS // 2
    for i in range(8):
        pay[i : i + 1, :] = (
            right[:, i * 128 : (i + 1) * 128]
            + 2.0 * right[:, half + i * 128 : half + (i + 1) * 128]
        )


def stage(binned, node, margin, labels, feature, cut):
    return pl.pallas_call(
        stage_kernel,
        out_shape=(
            jax.ShapeDtypeStruct((2 * NODES, ROWS), BF16),
            jax.ShapeDtypeStruct((FEATS, ROWS), F32),
            jax.ShapeDtypeStruct((16, 128), F32),
        ),
        in_specs=[VMEM] * 6,
        out_specs=[VMEM] * 3,
        scratch_shapes=[pltpu.VMEM((1, ROWS), F32)],
        name="stage",
        cost_estimate=cost(2 * 96 * ROWS * FEATS, 3 << 20),
    )(binned, node, margin, labels, feature, cut)


def histogram_kernel(weights, columns, send, keep):
    bins = bins_tile()

    def feature(f, carry):
        sums = bin_sums(
            weights, lambda k: columns[pl.ds(f, 1), k * TILE : (k + 1) * TILE], bins
        ).astype(BF16)
        send[f] = sums[:NODES]
        keep[f] = sums[NODES:]
        return carry

    lax.fori_loop(0, FEATS, feature, 0, unroll=4)


def histograms(weights, columns):
    half = jax.ShapeDtypeStruct((FEATS, NODES, BINS), BF16)
    return pl.pallas_call(
        histogram_kernel,
        out_shape=(half, half),
        in_specs=[VMEM] * 2,
        out_specs=[VMEM] * 2,
        name="histograms",
        cost_estimate=cost(2 * 64 * ROWS * FEATS * BINS, 3 << 20),
    )(weights, columns)


def chip_sum_kernel(keep, arrived, own, send):
    for f in range(0, FEATS, 8):
        total = keep[f : f + 8].astype(F32) + arrived[f : f + 8].astype(F32)
        own[f : f + 8] = total[:, :16]
        send[f : f + 8] = total[:, 16:].astype(BF16)


def chip_sum(keep, arrived):
    return pl.pallas_call(
        chip_sum_kernel,
        out_shape=(
            jax.ShapeDtypeStruct((FEATS, 16, BINS), F32),
            jax.ShapeDtypeStruct((FEATS, 16, BINS), BF16),
        ),
        in_specs=[VMEM] * 2,
        out_specs=[VMEM] * 2,
        name="chip_sum",
        cost_estimate=cost(FEATS * 32 * BINS, 3 << 20),
    )(keep, arrived)


def finish_kernel(
    own, arrived, parts, node, margin, labels, histogram, margin_out, child_out, grad_out, total
):
    for f in range(0, FEATS, 8):
        piece = (own[f : f + 8] + arrived[f : f + 8].astype(F32)).reshape(128, BINS)
        for h in range(2):
            total[h, f * 16 : (f + 8) * 16, :] = piece[:, h * 128 : (h + 1) * 128]
    for q in range(16):
        for h in range(2):
            histogram[q, :, h * 128 : (h + 1) * 128] = total[h, pl.ds(q, FEATS, stride=16), :]
    here = lax.axis_index("zl") * 2 + lax.axis_index("core")
    codes = parts[here, 0:8, :]
    for z in range(1, 4):
        codes = codes + parts[4 * z + here, 0:8, :]
    table = parts[0, 8:16, :]
    for m in range(1, 16):
        table = table + parts[m, 8:16, :]
    table = jnp.broadcast_to(table[0:1, :], (8, 128))
    rest = pltpu.roll(table, 64, 1) - table
    leaf_left = -table / (pltpu.roll(table, 127, 1) + 1.0)
    leaf_right = -rest / (pltpu.roll(rest, 127, 1) + 1.0)
    high = jnp.where(codes > 1.5, 1.0, 0.0)
    go_right = jnp.concatenate([codes - 2.0 * high, high], axis=0) > 0.5
    node_here = node[...]
    shift = jnp.zeros((16, 128), F32)
    for n in range(NODES):
        step = jnp.where(
            go_right,
            jnp.broadcast_to(leaf_right[0:1, 2 * n : 2 * n + 1], (16, 128)),
            jnp.broadcast_to(leaf_left[0:1, 2 * n : 2 * n + 1], (16, 128)),
        )
        shift = jnp.where(node_here == n, step, shift)
    moved = margin[...] + shift
    margin_out[...] = moved
    child_out[...] = 2 * node_here + jnp.where(go_right, 1, 0)
    fresh = jax.nn.sigmoid(moved)
    slope = fresh - labels[...]
    curve = fresh * (1.0 - fresh)
    for i in range(16):
        grad_out[0:1, i * 128 : (i + 1) * 128] = slope[i : i + 1, :]
        grad_out[1:2, i * 128 : (i + 1) * 128] = curve[i : i + 1, :]


def finish(own, arrived, parts, node, margin, labels):
    return pl.pallas_call(
        finish_kernel,
        out_shape=(
            jax.ShapeDtypeStruct((16, FEATS, BINS), F32),
            jax.ShapeDtypeStruct((16, 128), F32),
            jax.ShapeDtypeStruct((16, 128), jnp.int32),
            jax.ShapeDtypeStruct((2, ROWS), F32),
        ),
        in_specs=[VMEM] * 6,
        out_specs=[VMEM] * 4,
        scratch_shapes=[pltpu.VMEM((2, FEATS * 16, 128), F32)],
        name="finish",
        cost_estimate=cost(FEATS * 16 * BINS, 3 << 20),
    )(own, arrived, parts, node, margin, labels)


def share(part, axes, count):
    spread = jnp.broadcast_to(part[None], (count,) + part.shape)
    return lax.all_to_all(spread, axes, 0, 0, tiled=True)


def on_device(binned, node_of, margin, labels, split_feature, split_bin):
    swap = [(0, 1), (1, 0)]
    weights, columns, pay = stage(
        binned,
        node_of.reshape(1, ROWS),
        margin.reshape(1, ROWS),
        labels.reshape(1, ROWS),
        split_feature.reshape(1, NODES),
        split_bin.reshape(1, NODES),
    )
    send, keep = histograms(weights, columns)
    own, send_line = chip_sum(keep, lax.ppermute(send, "core", swap))
    arrived = lax.ppermute(send_line, "zl", swap)
    plane = jnp.sum(share(pay, PLANE, 32), axis=0)
    parts = share(plane, LINE, 16)
    histogram, margin_out, child_out, grad_out = finish(
        own,
        arrived,
        parts,
        node_of.reshape(16, 128),
        margin.reshape(16, 128),
        labels.reshape(16, 128),
    )
    return (
        histogram.reshape(8, 2, FEATS, BINS),
        margin_out.reshape(ROWS),
        child_out.reshape(ROWS),
        grad_out,
    )


def solution(mesh):
    fine = Mesh(mesh.devices.reshape(4, 8, 4, 2, 2), ("x", "y", "zh", "zl", "core"))
    rows = P(ROW_AXES)
    in_specs = (P(ROW_AXES, FEAT_AXES), rows, rows, rows, P(), P())
    out_specs = (P(ROW_AXES, None, FEAT_AXES, None), rows, rows, P(None, ROW_AXES))
    return jax.shard_map(
        on_device, mesh=fine, in_specs=in_specs, out_specs=out_specs, check_vma=False
    )
```

time: 511 us -> 80.6 us (0.16)
  the two profiles are of different devices: /device:TPU:64 before, /device:TPU:1 now
where the time goes in v1:
time: 80.6 us; the launch traced here: 80.2 us
  Pallas kernels  33.6 us (42%)
  blocking collectives  21.6 us (27%)
  starting transfers between devices  17.1 us (21%)
  local copies, waits for them, and re-layouts  4.85 us (6%)
  waiting for transfers between devices  2.37 us (3%)
    pallas_call x1, Pallas kernels, histograms(): pl.pallas_call(histogram_kernel, out_shape=(half, half), in_specs=[VMEM]...  24.7 us
    all_to_all x1, blocking collectives, share(): return lax.all_to_all(spread, axes, 0, 0, tiled=True)  21.6 us
    ppermute x1, starting transfers between devices, on_device(): own, send_line = chip_sum(keep, lax.ppermute(send, 'core', swap))  8.73 us
    all_to_all x1, starting transfers between devices, share(): return lax.all_to_all(spread, axes, 0, 0, tiled=True)  4.32 us
    unnamed x7, local copies, waits for them, and re-layouts  4.12 us
    ppermute x1, starting transfers between devices, on_device(): arrived = lax.ppermute(send_line, 'zl', swap)  3.99 us
    pallas_call x1, Pallas kernels, finish(): pl.pallas_call(finish_kernel, out_shape=(jax.ShapeDtypeStruct((16, FEATS,...  3.11 us
    pallas_call x1, Pallas kernels, chip_sum(): pl.pallas_call(chip_sum_kernel, out_shape=(jax.ShapeDtypeStruct((FEATS, 1...  2.93 us
  transfers between devices with their start and end apart: 3, of which 1 were waited for; matrix products, arithmetic and copies ran while one was open for 1% of the time, Pallas kernels for 4%

profile of v1, /device:TPU:1, one launch (start us, length us, event | category | flops | bytes accessed | tf_op | source)
XLA Modules:
  0.0 80.2 jit_solution(3109808764224404605)
XLA Ops:
  0.6 2.4 %copy.11.binned = s32[2048,64]{1,0:T(8,128)} copy(s32[2048,64]{0,1:T(8,128)} %param.6) | data formatting | bytes 1048576 | tf_op args[0]
  3.0 2.9 %stage.1 = (bf16[64,2048]{1,0:T(8,128)(2,1)}, f32[64,2048]{1,0:T(8,128)}, f32[16,128]{1,0:T(8,128)}) custom-call(s32[2048,64]{1,0:T(8,128)} %copy.11.binned, s32[1,2048]{1,0:T(1,128)} %bitcast.11, f32[1,2048]{1,0:T(1,128)} %bitcast.13, f32[1,2048]{1,0:T(1,128)} %bitcast.15, s32[1,32]{1,0:T(1,128)} %bitcast.17, s32[1,32]{1,0:T(1,128)} %bitcast.18), custom_call_target="tpu_custom_call" | custom-call | flops 25165824 | bytes 3145728 | tf_op jit(solution)/shard_map/stage/pallas_call | solution.py:109
  5.9 0.0 copy-start.2
  5.9 24.7 %histograms.1 = (bf16[64,32,256]{2,1,0:T(8,128)(2,1)}, bf16[64,32,256]{2,1,0:T(8,128)(2,1)}) custom-call(bf16[64,2048]{1,0:T(8,128)(2,1)} %get-tuple-element.15.weights, f32[64,2048]{1,0:T(8,128)} %get-tuple-element.16.columns), custom_call_target="tpu_custom_call" | custom-call | flops 4294967296 | bytes 3145728 | tf_op jit(solution)/shard_map/histograms/pallas_call | solution.py:140
  30.6 8.7 %collective-permute-start = (bf16[64,32,256]{2,1,0:T(8,128)(2,1)}, bf16[64,32,256]{2,1,0:T(8,128)(2,1)S(1)}, u32[]{:S(2)}, u32[]{:S(2)}) collective-permute-start(bf16[64,32,256]{2,1,0:T(8,128)(2,1)} %get-tuple-element.18), channel_id=1, source_target_pairs={{0,1},{1,0},{2,3},{3,2},{4,5},{5,4},{6,7},{7,6},{8,9},{9,8},{10,11... | collective-permute-start | bytes 3145736 | tf_op jit(solution)/shard_map/ppermute | solution.py:247
  39.3 0.0 copy-done.2
  39.3 0.7 broadcast_in_dim.4
  40.0 4.3 %all-to-all-start = ((f32[32,16,128]{2,1,0:T(8,128)}), f32[32,16,128]{2,1,0:T(8,128)S(1)}, u32[]{:S(2)}, u32[]{:S(2)}) async-start(f32[32,16,128]{2,1,0:T(8,128)} %broadcast_in_dim.4), calls=%async_computation | async-start | bytes 524288 | tf_op jit(solution)/shard_map/all_to_all | solution.py:233
  44.4 0.0 collective-permute-done.arrived
  44.4 0.0 copy-start
  44.4 1.0 %copy-done = bf16[64,32,256]{2,1,0:T(8,128)(2,1)} copy-done((bf16[64,32,256]{2,1,0:T(8,128)(2,1)}, bf16[64,32,256]{2,1,0:T(8,128)(2,1)S(1)}, u32[]{:S(2)}) %copy-start) | copy-done | bytes 1048600
  45.3 2.9 %chip_sum.1 = (f32[64,16,256]{2,1,0:T(8,128)}, bf16[64,16,256]{2,1,0:T(8,128)(2,1)}) custom-call(bf16[64,32,256]{2,1,0:T(8,128)(2,1)} %get-tuple-element.17.keep, bf16[64,32,256]{2,1,0:T(8,128)(2,1)} %copy-done), custom_call_target="tpu_custom_call" | custom-call | flops 524288 | bytes 3145728 | tf_op jit(solution)/shard_map/chip_sum/pallas_call | solution.py:158
  48.3 4.0 %collective-permute-start.1 = (bf16[64,16,256]{2,1,0:T(8,128)(2,1)}, bf16[64,16,256]{2,1,0:T(8,128)(2,1)S(1)}, u32[]{:S(2)}, u32[]{:S(2)}) collective-permute-start(bf16[64,16,256]{2,1,0:T(8,128)(2,1)} %get-tuple-element.20), channel_id=1, source_target_pairs={{0,2},{2,0},{1,3},{3,1},{4,6},{6,4},{5,7},{7,5},{8,10},{10,8},{9,1... | collective-permute-start | bytes 1572872 | tf_op jit(solution)/shard_map/ppermute | solution.py:248
  52.3 2.4 %all-to-all-done = f32[32,16,128]{2,1,0:T(8,128)S(1)} async-done(((f32[32,16,128]{2,1,0:T(8,128)}), f32[32,16,128]{2,1,0:T(8,128)S(1)}, u32[]{:S(2)}, u32[]{:S(2)}) %all-to-all-start) | async-done | bytes 262176 | tf_op jit(solution)/shard_map/all_to_all | solution.py:233
  54.7 21.6 %all_to_all.10.parts = f32[16,16,128]{2,1,0:T(8,128)} all-to-all(f32[16,16,128]{2,1,0:T(8,128)S(1)} %broadcast_in_dim.5), channel_id=1, replica_groups=mesh['x'=4,'y'=8,'zh'=4,'zl'=2,'core'=2] {'zh','zl','core'}, dimensions={0} | all-to-all | bytes 262144 | tf_op jit(solution)/shard_map/all_to_all | solution.py:233
  76.3 0.0 collective-permute-done.1.arrived
  76.3 0.0 copy-start.1
  76.3 0.8 copy-done.1
  77.1 3.1 %finish.1 = (f32[16,64,256]{2,1,0:T(8,128)}, f32[16,128]{1,0:T(8,128)}, s32[16,128]{1,0:T(8,128)}, f32[2,2048]{1,0:T(2,128)}) custom-call(f32[64,16,256]{2,1,0:T(8,128)} %get-tuple-element.19.own, bf16[64,16,256]{2,1,0:T(8,128)(2,1)} %copy-done.1, f32[16,16,128]{2,1,0:T(8,128)} %all_to_all.10.parts, s32[16,128]{1,0:T(8,128)} %bitcast.12, ...), custom_call_target="tpu_custom_call" | custom-call | flops 262144 | bytes 3145728 | tf_op jit(solution)/shard_map/finish/pallas_call | solution.py:215
  (2 shorter events, 0.0 us)
Async XLA Ops:
  5.9 33.4 %copy-start.2 = (f32[16,128]{1,0:T(8,128)S(1)}, f32[16,128]{1,0:T(8,128)}, u32[]{:S(2)}) copy-start(f32[16,128]{1,0:T(8,128)} %get-tuple-element.21) | copy-start | bytes 24580
  30.6 13.8 %collective-permute-start = (bf16[64,32,256]{2,1,0:T(8,128)(2,1)}, bf16[64,32,256]{2,1,0:T(8,128)(2,1)S(1)}, u32[]{:S(2)}, u32[]{:S(2)}) collective-permute-start(bf16[64,32,256]{2,1,0:T(8,128)(2,1)} %get-tuple-element.18), channel_id=1, source_target_pairs={{0,1},{1,0},{2,3},{3,2},{4,5},{5,4},{6,7},{7,6},{8,9},{9,8},{10,11... | collective-permute-start | bytes 3145736 | tf_op jit(solution)/shard_map/ppermute | solution.py:247
  40.0 14.6 %all-to-all-start = ((f32[32,16,128]{2,1,0:T(8,128)}), f32[32,16,128]{2,1,0:T(8,128)S(1)}, u32[]{:S(2)}, u32[]{:S(2)}) async-start(f32[32,16,128]{2,1,0:T(8,128)} %broadcast_in_dim.4), calls=%async_computation | async-start | bytes 524288 | tf_op jit(solution)/shard_map/all_to_all | solution.py:233
  44.4 1.0 %copy-start = (bf16[64,32,256]{2,1,0:T(8,128)(2,1)}, bf16[64,32,256]{2,1,0:T(8,128)(2,1)S(1)}, u32[]{:S(2)}) copy-start(bf16[64,32,256]{2,1,0:T(8,128)(2,1)S(1)} %collective-permute-done.arrived) | copy-start | bytes 3145732
  48.3 28.0 %collective-permute-start.1 = (bf16[64,16,256]{2,1,0:T(8,128)(2,1)}, bf16[64,16,256]{2,1,0:T(8,128)(2,1)S(1)}, u32[]{:S(2)}, u32[]{:S(2)}) collective-permute-start(bf16[64,16,256]{2,1,0:T(8,128)(2,1)} %get-tuple-element.20), channel_id=1, source_target_pairs={{0,2},{2,0},{1,3},{3,1},{4,6},{6,4},{5,7},{7,5},{8,10},{10,8},{9,1... | collective-permute-start | bytes 1572872 | tf_op jit(solution)/shard_map/ppermute | solution.py:248
  76.3 0.8 %copy-start.1 = (bf16[64,16,256]{2,1,0:T(8,128)(2,1)}, bf16[64,16,256]{2,1,0:T(8,128)(2,1)S(1)}, u32[]{:S(2)}) copy-start(bf16[64,16,256]{2,1,0:T(8,128)(2,1)S(1)} %collective-permute-done.1.arrived) | copy-start | bytes 1572868

commit v2 on v1

--- a/solution.py
+++ b/solution.py
@@ -17,6 +17,8 @@
 LINE = ("zh", "zl", "core")
 F32 = jnp.float32
 BF16 = jnp.bfloat16
+I16 = jnp.int16
+LIMIT = pltpu.CompilerParams(vmem_limit_bytes=16 << 20)
 VMEM = pl.BlockSpec(memory_space=pltpu.VMEM)
 
 
@@ -32,25 +34,23 @@
     return lax.dot_general(a, b, (((1,), (1,)), ((), ())), preferred_element_type=F32)
 
 
-def bin_hot(row, bins):
-    col = jnp.broadcast_to(row, (16, TILE)).astype(BF16)
-    col = jnp.concatenate([col] * (BINS // 16), axis=0)
-    return jnp.where(bins == col, BF16(1), BF16(0))
-
-
-def bin_sums(weights_ref, row_of, bins):
+def bin_sums(weights, row_of):
+    low_ids = iota((BINS // 2, TILE), 0).astype(I16)
+    one, zero = BF16(1), BF16(0)
     total = None
     for k in range(ROWS // TILE):
-        piece = contract_last(weights_ref[:, k * TILE : (k + 1) * TILE], bin_hot(row_of(k), bins))
+        row = jnp.broadcast_to(row_of(k), (16, TILE))
+        low = jnp.concatenate([(row & 127).astype(I16)] * 8, axis=0)
+        high = jnp.concatenate([(row >> 7).astype(I16)] * 4, axis=0)
+        tile = weights[:, k * TILE : (k + 1) * TILE]
+        split = [jnp.where(high == h, tile, zero) for h in range(2)]
+        hot = jnp.where(low_ids == low, one, zero)
+        piece = contract_last(jnp.concatenate(split, axis=0), hot)
         total = piece if total is None else total + piece
     return total
 
 
-def bins_tile():
-    return iota((BINS, TILE), 0).astype(F32).astype(BF16)
-
-
-def stage_kernel(binned, node, margin, labels, feature, cut, weights, columns, pay, chosen):
+def stage_kernel(columns, node, margin, labels, feature, cut, weights, pay, chosen):
     here = lax.axis_index("zl") * 2 + lax.axis_index("core")
     feat_start = (
         (lax.axis_index("x") * 8 + lax.axis_index("y")) * 4 + lax.axis_index("zh")
@@ -70,22 +70,18 @@
     local_n = jnp.sum(jnp.where(diagonal, local, 0), axis=1, keepdims=True)
     cut_n = jnp.sum(jnp.where(diagonal, cut[...], 0), axis=1, keepdims=True)
     owned_n = (local_n >= 0) & (local_n < FEATS)
-    picker = jnp.where(
-        iota((FEATS, FEATS), 0) == iota((FEATS, FEATS), 1), 1.0, 0.0
-    ).astype(BF16)
     chooser = jnp.where(iota((NODES, FEATS), 1) == local_n, 1.0, 0.0).astype(BF16)
-    table_bf = binned[...].astype(F32).astype(BF16)
-    columns[...] = contract_last(picker, table_bf)
-    split_values = contract_last(chooser, table_bf)
+    split_values = jnp.dot(
+        chooser, columns[...].astype(F32).astype(BF16), preferred_element_type=F32
+    )
     hot = node[...] == iota((NODES, ROWS), 0)
     value = jnp.sum(jnp.where(hot, split_values, 0.0), axis=0, keepdims=True)
     owned = jnp.sum(jnp.where(hot & owned_n, 1.0, 0.0), axis=0, keepdims=True)
     row_cut = jnp.sum(jnp.where(hot, cut_n.astype(F32), 0.0), axis=0, keepdims=True)
     right = jnp.where(value > row_cut, owned, 0.0)
-    chosen[...] = jnp.where(owned > 0.5, value, -1.0)
-    bins = bins_tile()
-    sums = bin_sums(weights, lambda k: chosen[:, k * TILE : (k + 1) * TILE], bins)
-    sums = sums.astype(BF16).astype(F32)
+    chosen[...] = jnp.where(owned > 0.5, value, -1.0).astype(jnp.int32)
+    sums = bin_sums(weights, lambda k: chosen[:, k * TILE : (k + 1) * TILE])
+    sums = jnp.concatenate([sums[:64], sums[64:]], axis=1).astype(BF16).astype(F32)
     cut_q = jnp.sum(
         jnp.where(iota((2 * NODES, NODES), 1) == node_q, cut[...], 0), axis=1, keepdims=True
     )
@@ -105,44 +101,45 @@
         )
 
 
-def stage(binned, node, margin, labels, feature, cut):
+def stage(columns, node, margin, labels, feature, cut):
     return pl.pallas_call(
         stage_kernel,
         out_shape=(
-            jax.ShapeDtypeStruct((2 * NODES, ROWS), BF16),
-            jax.ShapeDtypeStruct((FEATS, ROWS), F32),
-            jax.ShapeDtypeStruct((16, 128), F32),
+            pltpu.VMEM((2 * NODES, ROWS), BF16),
+            pltpu.VMEM((16, 128), F32),
         ),
         in_specs=[VMEM] * 6,
-        out_specs=[VMEM] * 3,
-        scratch_shapes=[pltpu.VMEM((1, ROWS), F32)],
+        out_specs=[VMEM] * 2,
+        scratch_shapes=[pltpu.VMEM((1, ROWS), jnp.int32)],
         name="stage",
+        compiler_params=LIMIT,
         cost_estimate=cost(2 * 96 * ROWS * FEATS, 3 << 20),
-    )(binned, node, margin, labels, feature, cut)
+    )(columns, node, margin, labels, feature, cut)
 
 
 def histogram_kernel(weights, columns, send, keep):
-    bins = bins_tile()
-
     def feature(f, carry):
         sums = bin_sums(
-            weights, lambda k: columns[pl.ds(f, 1), k * TILE : (k + 1) * TILE], bins
+            weights, lambda k: columns[pl.ds(f, 1), k * TILE : (k + 1) * TILE]
         ).astype(BF16)
-        send[f] = sums[:NODES]
-        keep[f] = sums[NODES:]
+        for h in range(2):
+            span = slice(h * 128, (h + 1) * 128)
+            send[f, :, span] = sums[64 * h : 64 * h + NODES]
+            keep[f, :, span] = sums[64 * h + NODES : 64 * h + 64]
         return carry
 
-    lax.fori_loop(0, FEATS, feature, 0, unroll=4)
+    lax.fori_loop(0, FEATS, feature, 0, unroll=8)
 
 
 def histograms(weights, columns):
-    half = jax.ShapeDtypeStruct((FEATS, NODES, BINS), BF16)
+    half = pltpu.VMEM((FEATS, NODES, BINS), BF16)
     return pl.pallas_call(
         histogram_kernel,
         out_shape=(half, half),
         in_specs=[VMEM] * 2,
         out_specs=[VMEM] * 2,
         name="histograms",
+        compiler_params=LIMIT,
         cost_estimate=cost(2 * 64 * ROWS * FEATS * BINS, 3 << 20),
     )(weights, columns)
 
@@ -158,12 +155,13 @@
     return pl.pallas_call(
         chip_sum_kernel,
         out_shape=(
-            jax.ShapeDtypeStruct((FEATS, 16, BINS), F32),
-            jax.ShapeDtypeStruct((FEATS, 16, BINS), BF16),
+            pltpu.VMEM((FEATS, 16, BINS), F32),
+            pltpu.VMEM((FEATS, 16, BINS), BF16),
         ),
         in_specs=[VMEM] * 2,
         out_specs=[VMEM] * 2,
         name="chip_sum",
+        compiler_params=LIMIT,
         cost_estimate=cost(FEATS * 32 * BINS, 3 << 20),
     )(keep, arrived)
 
@@ -224,6 +222,7 @@
         out_specs=[VMEM] * 4,
         scratch_shapes=[pltpu.VMEM((2, FEATS * 16, 128), F32)],
         name="finish",
+        compiler_params=LIMIT,
         cost_estimate=cost(FEATS * 16 * BINS, 3 << 20),
     )(own, arrived, parts, node, margin, labels)
 
@@ -233,21 +232,28 @@
     return lax.all_to_all(spread, axes, 0, 0, tiled=True)
 
 
+def near(array):
+    return pltpu.with_memory_space_constraint(array, pltpu.VMEM)
+
+
 def on_device(binned, node_of, margin, labels, split_feature, split_bin):
     swap = [(0, 1), (1, 0)]
-    weights, columns, pay = stage(
-        binned,
+    columns = binned.T
+    weights, pay = stage(
+        columns,
         node_of.reshape(1, ROWS),
         margin.reshape(1, ROWS),
         labels.reshape(1, ROWS),
         split_feature.reshape(1, NODES),
         split_bin.reshape(1, NODES),
     )
-    send, keep = histograms(weights, columns)
-    own, send_line = chip_sum(keep, lax.ppermute(send, "core", swap))
+    plane = share(pay, PLANE, 32)
+    send, keep = histograms(near(weights), columns)
+    parts = share(jnp.sum(plane, axis=0), LINE, 16)
+    arrived = lax.ppermute(send, "core", swap)
+    own, send_line = chip_sum(near(keep), near(arrived))
     arrived = lax.ppermute(send_line, "zl", swap)
-    plane = jnp.sum(share(pay, PLANE, 32), axis=0)
-    parts = share(plane, LINE, 16)
+    own, arrived, parts = near(own), near(arrived), near(parts)
     histogram, margin_out, child_out, grad_out = finish(
         own,
         arrived,
@@ -269,6 +275,7 @@
     rows = P(ROW_AXES)
     in_specs = (P(ROW_AXES, FEAT_AXES), rows, rows, rows, P(), P())
     out_specs = (P(ROW_AXES, None, FEAT_AXES, None), rows, rows, P(None, ROW_AXES))
+
     return jax.shard_map(
         on_device, mesh=fine, in_specs=in_specs, out_specs=out_specs, check_vma=False
     )

time: 80.6 us -> 62.3 us (0.77)
  Pallas kernels: 33.6 us -> 13.4 us
  waiting for transfers between devices: 2.37 us -> 5.33 us
  local copies, waits for them, and re-layouts: 4.85 us -> 3.85 us
    pallas_call x1, Pallas kernels: 24.7 us -> 10 us  [histograms(): pl.pallas_call(histogram_kernel, out_shape=(half, half), in_specs=[VMEM]...]
    pallas_call x2, Pallas kernels: 5.83 us -> 1.64 us  [the longest x1 0.95 us: chip_sum(): pl.pallas_call(chip_sum_kernel, out_shape=(pltpu.VMEM((FEATS, 16, BINS),...]
    all_to_all x1, waiting for transfers between devices: 2.37 us -> 5.33 us  [share(): return lax.all_to_all(spread, axes, 0, 0, tiled=True)]
    pallas_call x1, Pallas kernels: 3.11 us -> 1.7 us  [finish(): pl.pallas_call(finish_kernel, out_shape=(jax.ShapeDtypeStruct((16, FEATS,...]
    unnamed x7 -> x16, local copies, waits for them, and re-layouts: 4.12 us -> 3.13 us
  transfers between devices with their start and end apart: 3 -> 3, of which waited for: 1 -> 1; matrix products, arithmetic and copies ran while one was open for 1% -> 1% of each run, Pallas kernels for 4% -> 2%
where the time goes in v2:
time: 62.3 us; the launch traced here: 61.9 us
  blocking collectives  21.5 us (35%)
  starting transfers between devices  17.1 us (27%)
  Pallas kernels  13.4 us (22%)
  waiting for transfers between devices  5.33 us (9%)
  local copies, waits for them, and re-layouts  3.85 us (6%)
  between operations  0.74 us (1%)
    all_to_all x1, blocking collectives, share(): return lax.all_to_all(spread, axes, 0, 0, tiled=True)  21.5 us
    pallas_call x1, Pallas kernels, histograms(): pl.pallas_call(histogram_kernel, out_shape=(half, half), in_specs=[VMEM]...  10 us
    ppermute x1, starting transfers between devices, on_device(): arrived = lax.ppermute(send, 'core', swap)  8.75 us
    all_to_all x1, waiting for transfers between devices, share(): return lax.all_to_all(spread, axes, 0, 0, tiled=True)  5.33 us
    all_to_all x1, starting transfers between devices, share(): return lax.all_to_all(spread, axes, 0, 0, tiled=True)  4.33 us
    ppermute x1, starting transfers between devices, on_device(): arrived = lax.ppermute(send_line, 'zl', swap)  3.99 us
    unnamed x16, local copies, waits for them, and re-layouts  3.13 us
    pallas_call x1, Pallas kernels, finish(): pl.pallas_call(finish_kernel, out_shape=(jax.ShapeDtypeStruct((16, FEATS,...  1.7 us
  transfers between devices with their start and end apart: 3, of which 1 were waited for; matrix products, arithmetic and copies ran while one was open for 1% of the time, Pallas kernels for 2%

profile of v2, /device:TPU:1, one launch (start us, length us, event | category | flops | bytes accessed | tf_op | source)
XLA Modules:
  0.0 61.9 jit_solution(14809127486338196396)
XLA Ops:
  0.6 0.0 copy-start.1
  0.6 0.0 copy-start.6
  0.7 0.0 copy-start.7
  0.7 0.7 %copy-done.1 = s32[2048]{0:T(1024)S(1)} copy-done((s32[2048]{0:T(1024)S(1)}, s32[2048]{0:T(1024)}, u32[]{:S(2)}) %copy-start.1) | copy-done | bytes 8216
  1.3 0.0 copy-done.6
  1.3 0.0 copy-done.7
  1.3 0.0 copy-start
  1.3 1.0 %copy-done = s32[2048,64]{0,1:T(8,128)S(1)} copy-done((s32[2048,64]{0,1:T(8,128)S(1)}, s32[2048,64]{0,1:T(8,128)}, u32[]{:S(2)}) %copy-start) | copy-done | bytes 524312
  2.4 0.0 copy-start.2
  2.4 0.7 %copy-done.2 = f32[2048]{0:T(1024)S(1)} copy-done((f32[2048]{0:T(1024)S(1)}, f32[2048]{0:T(1024)}, u32[]{:S(2)}) %copy-start.2) | copy-done | bytes 8216
  3.1 0.0 copy-start.4
  3.1 0.7 %copy-done.4 = f32[2048]{0:T(1024)S(1)} copy-done((f32[2048]{0:T(1024)S(1)}, f32[2048]{0:T(1024)}, u32[]{:S(2)}) %copy-start.4) | copy-done | bytes 8216
  3.8 0.7 %stage.1 = (bf16[64,2048]{1,0:T(8,128)(2,1)S(1)}, f32[16,128]{1,0:T(8,128)S(1)}) custom-call(s32[64,2048]{1,0:T(8,128)S(1)} %bitcast.12, s32[1,2048]{1,0:T(1,128)S(1)} %bitcast.14, f32[1,2048]{1,0:T(1,128)S(1)} %bitcast.16, f32[1,2048]{1,0:T(1,128)S(1)} %bitcast.18, s32[1,32]{1,0:T(1,128)S(1)} %bitcast.20, s32[1,32]{1,0:T(1,128)S(1)} %bitcast.21), custom_call_target="tpu_custom_call" | custom-call | flops 25165824 | bytes 3145728 | tf_op jit(solution)/shard_map/stage/pallas_call | solution.py:105
  4.5 10.0 %histograms.1 = (bf16[64,32,256]{2,1,0:T(8,128)(2,1)S(1)}, bf16[64,32,256]{2,1,0:T(8,128)(2,1)S(1)}) custom-call(bf16[64,2048]{1,0:T(8,128)(2,1)S(1)} %get-tuple-element.14.weights, s32[64,2048]{1,0:T(8,128)S(1)} %bitcast.13), custom_call_target="tpu_custom_call" | custom-call | flops 4294967296 | bytes 3145728 | tf_op jit(solution)/shard_map/histograms/pallas_call | solution.py:136
  14.5 8.7 %collective-permute-start = (bf16[64,32,256]{2,1,0:T(8,128)(2,1)S(1)}, bf16[64,32,256]{2,1,0:T(8,128)(2,1)S(1)}, u32[]{:S(2)}, u32[]{:S(2)}) collective-permute-start(bf16[64,32,256]{2,1,0:T(8,128)(2,1)S(1)} %get-tuple-element.16), channel_id=1, source_target_pairs={{0,1},{1,0},{2,3},{3,2},{4,5},{5,4},{6,7},{7,6},{8,9},{9,8},{10,11... | collective-permute-start | bytes 3145736 | tf_op jit(solution)/shard_map/ppermute | solution.py:253
  23.3 0.7 %broadcast_in_dim.4 = f32[32,16,128]{2,1,0:T(8,128)} broadcast(f32[16,128]{1,0:T(8,128)S(1)} %get-tuple-element.19), dimensions={1,2} | broadcast | bytes 270336 | tf_op jit(solution)/shard_map/broadcast_in_dim | solution.py:231
  24.0 4.3 %all-to-all-start = ((f32[32,16,128]{2,1,0:T(8,128)}), f32[32,16,128]{2,1,0:T(8,128)S(1)}, u32[]{:S(2)}, u32[]{:S(2)}) async-start(f32[32,16,128]{2,1,0:T(8,128)} %broadcast_in_dim.4), calls=%async_computation | async-start | bytes 524288 | tf_op jit(solution)/shard_map/all_to_all | solution.py:232
  28.3 0.0 collective-permute-done.arrived
  28.3 0.9 %chip_sum.1 = (f32[64,16,256]{2,1,0:T(8,128)S(1)}, bf16[64,16,256]{2,1,0:T(8,128)(2,1)}) custom-call(bf16[64,32,256]{2,1,0:T(8,128)(2,1)S(1)} %get-tuple-element.15.keep, bf16[64,32,256]{2,1,0:T(8,128)(2,1)S(1)} %collective-permute-done.arrived), custom_call_target="tpu_custom_call" | custom-call | flops 524288 | bytes 3145728 | tf_op jit(solution)/shard_map/chip_sum/pallas_call | solution.py:155
  29.3 4.0 %collective-permute-start.1 = (bf16[64,16,256]{2,1,0:T(8,128)(2,1)}, bf16[64,16,256]{2,1,0:T(8,128)(2,1)S(1)}, u32[]{:S(2)}, u32[]{:S(2)}) collective-permute-start(bf16[64,16,256]{2,1,0:T(8,128)(2,1)} %get-tuple-element.18), channel_id=1, source_target_pairs={{0,2},{2,0},{1,3},{3,1},{4,6},{6,4},{5,7},{7,5},{8,10},{10,8},{9,1... | collective-permute-start | bytes 1572872 | tf_op jit(solution)/shard_map/ppermute | solution.py:255
  33.3 5.3 %all-to-all-done = f32[32,16,128]{2,1,0:T(8,128)S(1)} async-done(((f32[32,16,128]{2,1,0:T(8,128)}), f32[32,16,128]{2,1,0:T(8,128)S(1)}, u32[]{:S(2)}, u32[]{:S(2)}) %all-to-all-start) | async-done | bytes 262176 | tf_op jit(solution)/shard_map/all_to_all | solution.py:232
  38.6 0.0 copy-start.3
  38.7 0.0 copy-start.5
  38.7 21.5 %all_to_all.10.parts = f32[16,16,128]{2,1,0:T(8,128)S(1)} all-to-all(f32[16,16,128]{2,1,0:T(8,128)S(1)} %broadcast_in_dim.5), channel_id=1, replica_groups=mesh['x'=4,'y'=8,'zh'=4,'zl'=2,'core'=2] {'zh','zl','core'}, dimensions={0} | all-to-all | bytes 262144 | tf_op jit(solution)/shard_map/all_to_all | solution.py:232
  60.2 0.0 collective-permute-done.1.arrived
  60.2 0.0 copy-done.3
  60.2 0.0 copy-done.5
  60.2 1.7 %finish.1 = (f32[16,64,256]{2,1,0:T(8,128)}, f32[16,128]{1,0:T(8,128)}, s32[16,128]{1,0:T(8,128)}, f32[2,2048]{1,0:T(2,128)}) custom-call(f32[64,16,256]{2,1,0:T(8,128)S(1)} %get-tuple-element.17.own, bf16[64,16,256]{2,1,0:T(8,128)(2,1)S(1)} %collective-permute-done.1.arrived, f32[16,16,128]{2,1,0:T(8,128)S(1)} %all_to_all.10.parts, s32[16,128]{1,0:T(8,128)S(1)} %bitcast.15, ...), custom_call_target="tpu_custom_call" | custom-call | flops 262144 | bytes 3145728 | tf_op jit(solution)/shard_map/finish/pallas_call | solution.py:213
  (2 shorter events, 0.0 us)
Async XLA Ops:
  0.6 0.7 %copy-start.1 = (s32[2048]{0:T(1024)S(1)}, s32[2048]{0:T(1024)}, u32[]{:S(2)}) copy-start(s32[2048]{0:T(1024)} %param.7) | copy-start | bytes 24580
  0.6 0.7 %copy-start.6 = (s32[32]{0:T(128)S(1)}, s32[32]{0:T(128)}, u32[]{:S(2)}) copy-start(s32[32]{0:T(128)} %param.10) | copy-start | bytes 388
  0.7 0.7 %copy-start.7 = (s32[32]{0:T(128)S(1)}, s32[32]{0:T(128)}, u32[]{:S(2)}) copy-start(s32[32]{0:T(128)} %param.11) | copy-start | bytes 388
  1.3 1.0 %copy-start = (s32[2048,64]{0,1:T(8,128)S(1)}, s32[2048,64]{0,1:T(8,128)}, u32[]{:S(2)}) copy-start(s32[2048,64]{0,1:T(8,128)} %param.6) | copy-start | bytes 1572868
  2.4 0.7 %copy-start.2 = (f32[2048]{0:T(1024)S(1)}, f32[2048]{0:T(1024)}, u32[]{:S(2)}) copy-start(f32[2048]{0:T(1024)} %param.8) | copy-start | bytes 24580
  3.1 0.7 %copy-start.4 = (f32[2048]{0:T(1024)S(1)}, f32[2048]{0:T(1024)}, u32[]{:S(2)}) copy-start(f32[2048]{0:T(1024)} %param.9) | copy-start | bytes 24580
  14.5 13.8 %collective-permute-start = (bf16[64,32,256]{2,1,0:T(8,128)(2,1)S(1)}, bf16[64,32,256]{2,1,0:T(8,128)(2,1)S(1)}, u32[]{:S(2)}, u32[]{:S(2)}) collective-permute-start(bf16[64,32,256]{2,1,0:T(8,128)(2,1)S(1)} %get-tuple-element.16), channel_id=1, source_target_pairs={{0,1},{1,0},{2,3},{3,2},{4,5},{5,4},{6,7},{7,6},{8,9},{9,8},{10,11... | collective-permute-start | bytes 3145736 | tf_op jit(solution)/shard_map/ppermute | solution.py:253
  24.0 14.6 %all-to-all-start = ((f32[32,16,128]{2,1,0:T(8,128)}), f32[32,16,128]{2,1,0:T(8,128)S(1)}, u32[]{:S(2)}, u32[]{:S(2)}) async-start(f32[32,16,128]{2,1,0:T(8,128)} %broadcast_in_dim.4), calls=%async_computation | async-start | bytes 524288 | tf_op jit(solution)/shard_map/all_to_all | solution.py:232
  29.3 30.9 %collective-permute-start.1 = (bf16[64,16,256]{2,1,0:T(8,128)(2,1)}, bf16[64,16,256]{2,1,0:T(8,128)(2,1)S(1)}, u32[]{:S(2)}, u32[]{:S(2)}) collective-permute-start(bf16[64,16,256]{2,1,0:T(8,128)(2,1)} %get-tuple-element.18), channel_id=1, source_target_pairs={{0,2},{2,0},{1,3},{3,1},{4,6},{6,4},{5,7},{7,5},{8,10},{10,8},{9,1... | collective-permute-start | bytes 1572872 | tf_op jit(solution)/shard_map/ppermute | solution.py:255
  38.6 21.5 %copy-start.3 = (f32[2048]{0:T(1024)S(1)}, f32[2048]{0:T(1024)}, u32[]{:S(2)}) copy-start(f32[2048]{0:T(1024)} %param.8) | copy-start | bytes 24580
  38.7 21.5 %copy-start.5 = (f32[2048]{0:T(1024)S(1)}, f32[2048]{0:T(1024)}, u32[]{:S(2)}) copy-start(f32[2048]{0:T(1024)} %param.9) | copy-start | bytes 24580

commit v3 on v2

--- a/solution.py
+++ b/solution.py
@@ -91,14 +91,15 @@
     lane = iota((2 * NODES, 128), 1)
     slot = 2 * node_q + channel
     entries = jnp.where(lane == slot, left, 0.0) + jnp.where(lane == slot + 64, whole, 0.0)
-    pay[...] = jnp.zeros((16, 128), F32)
-    pay[8:9, :] = jnp.sum(entries, axis=0, keepdims=True)
     half = ROWS // 2
-    for i in range(8):
-        pay[i : i + 1, :] = (
-            right[:, i * 128 : (i + 1) * 128]
-            + 2.0 * right[:, half + i * 128 : half + (i + 1) * 128]
-        )
+    lines = [
+        right[:, i * 128 : (i + 1) * 128] + 2.0 * right[:, half + i * 128 : half + (i + 1) * 128]
+        for i in range(8)
+    ]
+    lines.append(jnp.sum(entries, axis=0, keepdims=True))
+    for p in range(32):
+        for i in range(9):
+            pay[p, i] = lines[i]
 
 
 def stage(columns, node, margin, labels, feature, cut):
@@ -106,7 +107,7 @@
         stage_kernel,
         out_shape=(
             pltpu.VMEM((2 * NODES, ROWS), BF16),
-            pltpu.VMEM((16, 128), F32),
+            pltpu.VMEM((32, 9, 1, 128), F32),
         ),
         in_specs=[VMEM] * 6,
         out_specs=[VMEM] * 2,
@@ -166,9 +167,28 @@
     )(keep, arrived)
 
 
-def finish_kernel(
-    own, arrived, parts, node, margin, labels, histogram, margin_out, child_out, grad_out, total
-):
+def relay_kernel(plane, pay):
+    for i in range(9):
+        line = plane[0, i]
+        for p in range(1, 32):
+            line = line + plane[p, i]
+        for p in range(16):
+            pay[p, i] = line
+
+
+def relay(plane):
+    return pl.pallas_call(
+        relay_kernel,
+        out_shape=pltpu.VMEM((16, 9, 1, 128), F32),
+        in_specs=[VMEM],
+        out_specs=VMEM,
+        name="relay",
+        compiler_params=LIMIT,
+        cost_estimate=cost(32 * 9 * 128, 1 << 17),
+    )(plane)
+
+
+def finish_kernel(own, arrived, histogram, total):
     for f in range(0, FEATS, 8):
         piece = (own[f : f + 8] + arrived[f : f + 8].astype(F32)).reshape(128, BINS)
         for h in range(2):
@@ -176,14 +196,33 @@
     for q in range(16):
         for h in range(2):
             histogram[q, :, h * 128 : (h + 1) * 128] = total[h, pl.ds(q, FEATS, stride=16), :]
+
+
+def finish(own, arrived):
+    return pl.pallas_call(
+        finish_kernel,
+        out_shape=jax.ShapeDtypeStruct((16, FEATS, BINS), F32),
+        in_specs=[VMEM] * 2,
+        out_specs=VMEM,
+        scratch_shapes=[pltpu.VMEM((2, FEATS * 16, 128), F32)],
+        name="finish",
+        compiler_params=LIMIT,
+        cost_estimate=cost(FEATS * 16 * BINS, 3 << 20),
+    )(own, arrived)
+
+
+def rows_kernel(parts, node, margin, labels, margin_out, child_out, grad_out, codes_ref):
     here = lax.axis_index("zl") * 2 + lax.axis_index("core")
-    codes = parts[here, 0:8, :]
-    for z in range(1, 4):
-        codes = codes + parts[4 * z + here, 0:8, :]
-    table = parts[0, 8:16, :]
+    for i in range(8):
+        line = parts[here, i]
+        for z in range(1, 4):
+            line = line + parts[4 * z + here, i]
+        codes_ref[i : i + 1, :] = line
+    table = parts[0, 8]
     for m in range(1, 16):
-        table = table + parts[m, 8:16, :]
-    table = jnp.broadcast_to(table[0:1, :], (8, 128))
+        table = table + parts[m, 8]
+    codes = codes_ref[...]
+    table = jnp.broadcast_to(table, (8, 128))
     rest = pltpu.roll(table, 64, 1) - table
     leaf_left = -table / (pltpu.roll(table, 127, 1) + 1.0)
     leaf_right = -rest / (pltpu.roll(rest, 127, 1) + 1.0)
@@ -209,58 +248,59 @@
         grad_out[1:2, i * 128 : (i + 1) * 128] = curve[i : i + 1, :]
 
 
-def finish(own, arrived, parts, node, margin, labels):
-    return pl.pallas_call(
-        finish_kernel,
+def rows_update(parts, node, margin, labels):
+    return pl.pallas_call(
+        rows_kernel,
         out_shape=(
-            jax.ShapeDtypeStruct((16, FEATS, BINS), F32),
             jax.ShapeDtypeStruct((16, 128), F32),
             jax.ShapeDtypeStruct((16, 128), jnp.int32),
             jax.ShapeDtypeStruct((2, ROWS), F32),
         ),
-        in_specs=[VMEM] * 6,
-        out_specs=[VMEM] * 4,
-        scratch_shapes=[pltpu.VMEM((2, FEATS * 16, 128), F32)],
-        name="finish",
-        compiler_params=LIMIT,
-        cost_estimate=cost(FEATS * 16 * BINS, 3 << 20),
-    )(own, arrived, parts, node, margin, labels)
-
-
-def share(part, axes, count):
-    spread = jnp.broadcast_to(part[None], (count,) + part.shape)
+        in_specs=[VMEM] * 4,
+        out_specs=[VMEM] * 3,
+        scratch_shapes=[pltpu.VMEM((8, 128), F32)],
+        name="rows_update",
+        compiler_params=LIMIT,
+        cost_estimate=cost(ROWS * 128, 1 << 17),
+    )(parts, node, margin, labels)
+
+
+def share(spread, axes):
     return lax.all_to_all(spread, axes, 0, 0, tiled=True)
 
 
 def near(array):
     return pltpu.with_memory_space_constraint(array, pltpu.VMEM)
+
+
+def far(array):
+    return pltpu.with_memory_space_constraint(array, pltpu.HBM)
 
 
 def on_device(binned, node_of, margin, labels, split_feature, split_bin):
     swap = [(0, 1), (1, 0)]
     columns = binned.T
     weights, pay = stage(
-        columns,
-        node_of.reshape(1, ROWS),
-        margin.reshape(1, ROWS),
-        labels.reshape(1, ROWS),
-        split_feature.reshape(1, NODES),
-        split_bin.reshape(1, NODES),
-    )
-    plane = share(pay, PLANE, 32)
+        far(columns),
+        far(node_of.reshape(1, ROWS)),
+        far(margin.reshape(1, ROWS)),
+        far(labels.reshape(1, ROWS)),
+        far(split_feature.reshape(1, NODES)),
+        far(split_bin.reshape(1, NODES)),
+    )
+    plane = share(pay, PLANE)
     send, keep = histograms(near(weights), columns)
-    parts = share(jnp.sum(plane, axis=0), LINE, 16)
     arrived = lax.ppermute(send, "core", swap)
+    pay = relay(near(plane))
     own, send_line = chip_sum(near(keep), near(arrived))
     arrived = lax.ppermute(send_line, "zl", swap)
-    own, arrived, parts = near(own), near(arrived), near(parts)
-    histogram, margin_out, child_out, grad_out = finish(
-        own,
-        arrived,
-        parts,
-        node_of.reshape(16, 128),
-        margin.reshape(16, 128),
-        labels.reshape(16, 128),
+    parts = share(pay, LINE)
+    histogram = finish(near(own), near(arrived))
+    margin_out, child_out, grad_out = rows_update(
+        near(parts),
+        near(node_of.reshape(16, 128)),
+        near(margin.reshape(16, 128)),
+        near(labels.reshape(16, 128)),
     )
     return (
         histogram.reshape(8, 2, FEATS, BINS),

time: 62.3 us -> 63.5 us (1.019)
  blocking collectives: 21.5 us -> 35 us
  starting transfers between devices: 17.1 us -> 10.7 us
  local copies, waits for them, and re-layouts: 3.85 us -> 0.02 us
  waiting for transfers between devices: 5.33 us -> 2.27 us
  Pallas kernels: 13.4 us -> 14.6 us
    all_to_all x1 -> x2, blocking collectives: 21.5 us -> 35 us  [share(): return lax.all_to_all(spread, axes, 0, 0, tiled=True)]
    all_to_all x1 -> x0, waiting for transfers between devices: 5.33 us -> none  [share(): return lax.all_to_all(spread, axes, 0, 0, tiled=True)]
    all_to_all x1 -> x0, starting transfers between devices: 4.33 us -> none  [share(): return lax.all_to_all(spread, axes, 0, 0, tiled=True)]
    unnamed x16 -> x8, local copies, waits for them, and re-layouts: 3.13 us -> 0.02 us
    ppermute x1, waiting for transfers between devices: 0.01 us -> 2.26 us  [on_device(): arrived = lax.ppermute(send, 'core', swap)]
    ppermute x1, starting transfers between devices: 3.99 us -> 1.92 us  [on_device(): arrived = lax.ppermute(send_line, 'zl', swap)]
    pallas_call x1, Pallas kernels: 0.69 us -> 1.88 us  [stage(): pl.pallas_call(stage_kernel, out_shape=(pltpu.VMEM((2 * NODES, ROWS), BF1...]
    pallas_call x1 -> x3, Pallas kernels: 1.7 us -> 2.45 us  [the longest x1 1.39 us: finish(): pl.pallas_call(finish_kernel, out_shape=jax.ShapeDtypeStruct((16, FEATS,...]
  transfers between devices with their start and end apart: 3 -> 2, of which waited for: 1 -> 1; matrix products, arithmetic and copies ran while one was open for 1% -> 0% of each run, Pallas kernels for 2% -> 2%
where the time goes in v3:
time: 63.5 us; the launch traced here: 63.2 us
  blocking collectives  35 us (55%)
  Pallas kernels  14.6 us (23%)
  starting transfers between devices  10.7 us (17%)
  waiting for transfers between devices  2.27 us (4%)
  between operations  0.71 us (1%)
    all_to_all x2, blocking collectives, share(): return lax.all_to_all(spread, axes, 0, 0, tiled=True)  35 us
    pallas_call x1, Pallas kernels, histograms(): pl.pallas_call(histogram_kernel, out_shape=(half, half), in_specs=[VMEM]...  10 us
    ppermute x1, starting transfers between devices, on_device(): arrived = lax.ppermute(send, 'core', swap)  8.75 us
    ppermute x1, waiting for transfers between devices, on_device(): arrived = lax.ppermute(send, 'core', swap)  2.26 us
    ppermute x1, starting transfers between devices, on_device(): arrived = lax.ppermute(send_line, 'zl', swap)  1.92 us
    pallas_call x1, Pallas kernels, stage(): pl.pallas_call(stage_kernel, out_shape=(pltpu.VMEM((2 * NODES, ROWS), BF1...  1.88 us
    pallas_call x1, Pallas kernels, finish(): pl.pallas_call(finish_kernel, out_shape=jax.ShapeDtypeStruct((16, FEATS,...  1.39 us
  transfers between devices with their start and end apart: 2, of which 1 were waited for; matrix products, arithmetic and copies ran while one was open for 0% of the time, Pallas kernels for 2%

profile of v3, /device:TPU:1, one launch (start us, length us, event | category | flops | bytes accessed | tf_op | source)
XLA Modules:
  0.0 63.2 jit_solution(949544270183624763)
XLA Ops:
  0.6 0.0 copy-start
  0.6 1.9 %stage.1 = (bf16[64,2048]{1,0:T(8,128)(2,1)S(1)}, f32[32,9,1,128]{3,2,1,0:T(1,128)S(1)}) custom-call(s32[64,2048]{1,0:T(8,128)} %bitcast.12, s32[1,2048]{1,0:T(1,128)} %bitcast.14, f32[1,2048]{1,0:T(1,128)} %bitcast.16, f32[1,2048]{1,0:T(1,128)} %bitcast.18, s32[1,32]{1,0:T(1,128)} %bitcast.21, s32[1,32]{1,0:T(1,128)} %bitcast.22), custom_call_target="tpu_custom_call" | custom-call | flops 25165824 | bytes 3145728 | tf_op jit(solution)/shard_map/stage/pallas_call | solution.py:106
  2.5 0.0 copy-done
  2.5 10.0 %histograms.1 = (bf16[64,32,256]{2,1,0:T(8,128)(2,1)S(1)}, bf16[64,32,256]{2,1,0:T(8,128)(2,1)S(1)}) custom-call(bf16[64,2048]{1,0:T(8,128)(2,1)S(1)} %get-tuple-element.13.weights, s32[64,2048]{1,0:T(8,128)S(1)} %bitcast.13), custom_call_target="tpu_custom_call" | custom-call | flops 4294967296 | bytes 3145728 | tf_op jit(solution)/shard_map/histograms/pallas_call | solution.py:137
  12.6 8.7 %collective-permute-start = (bf16[64,32,256]{2,1,0:T(8,128)(2,1)S(1)}, bf16[64,32,256]{2,1,0:T(8,128)(2,1)S(1)}, u32[]{:S(2)}, u32[]{:S(2)}) collective-permute-start(bf16[64,32,256]{2,1,0:T(8,128)(2,1)S(1)} %get-tuple-element.15), channel_id=1, source_target_pairs={{0,1},{1,0},{2,3},{3,2},{4,5},{5,4},{6,7},{7,6},{8,9},{9,8},{10,11... | collective-permute-start | bytes 3145736 | tf_op jit(solution)/shard_map/ppermute | solution.py:293
  21.3 2.3 %collective-permute-done.arrived = bf16[64,32,256]{2,1,0:T(8,128)(2,1)S(1)} collective-permute-done((bf16[64,32,256]{2,1,0:T(8,128)(2,1)S(1)}, bf16[64,32,256]{2,1,0:T(8,128)(2,1)S(1)}, u32[]{:S(2)}, u32[]{:S(2)}) %collective-permute-start) | collective-permute-done | bytes 1048608 | tf_op jit(solution)/shard_map/ppermute | solution.py:293
  23.6 0.2 chip_sum.1
  23.8 1.9 %collective-permute-start.1 = (bf16[64,16,256]{2,1,0:T(8,128)(2,1)S(1)}, bf16[64,16,256]{2,1,0:T(8,128)(2,1)S(1)}, u32[]{:S(2)}, u32[]{:S(2)}) collective-permute-start(bf16[64,16,256]{2,1,0:T(8,128)(2,1)S(1)} %get-tuple-element.17), channel_id=1, source_target_pairs={{0,2},{2,0},{1,3},{3,1},{4,6},{6,4},{5,7},{7,5},{8,10},{10,8},{9,1... | collective-permute-start | bytes 1572872 | tf_op jit(solution)/shard_map/ppermute | solution.py:296
  25.7 15.5 %all_to_all.10.plane = f32[32,9,1,128]{3,2,1,0:T(1,128)S(1)} all-to-all(f32[32,9,1,128]{3,2,1,0:T(1,128)S(1)} %get-tuple-element.18), channel_id=1, replica_groups=mesh['x'=4,'y'=8,'zh'=4,'zl'=2,'core'=2] {'x','y'}, dimensions={0} | all-to-all | bytes 294912 | tf_op jit(solution)/shard_map/all_to_all | solution.py:269
  41.3 0.1 relay.1
  41.3 0.0 copy-start.1
  41.4 0.0 copy-start.2
  41.4 0.0 copy-start.3
  41.4 19.4 %all_to_all.11.parts = f32[16,9,1,128]{3,2,1,0:T(1,128)S(1)} all-to-all(f32[16,9,1,128]{3,2,1,0:T(1,128)S(1)} %relay.1), channel_id=1, replica_groups=mesh['x'=4,'y'=8,'zh'=4,'zl'=2,'core'=2] {'zh','zl','core'}, dimensions={0} | all-to-all | bytes 147456 | tf_op jit(solution)/shard_map/all_to_all | solution.py:269
  60.8 0.0 copy-done.1
  60.8 0.0 copy-done.2
  60.8 0.0 copy-done.3
  60.8 1.0 %rows_update.1 = (f32[16,128]{1,0:T(8,128)}, s32[16,128]{1,0:T(8,128)}, f32[2,2048]{1,0:T(2,128)}) custom-call(f32[16,9,1,128]{3,2,1,0:T(1,128)S(1)} %all_to_all.11.parts, s32[16,128]{1,0:T(8,128)S(1)} %bitcast.15, f32[16,128]{1,0:T(8,128)S(1)} %bitcast.17, f32[16,128]{1,0:T(8,128)S(1)} %bitcast.19), custom_call_target="tpu_custom_call" | custom-call | flops 262144 | bytes 131072 | tf_op jit(solution)/shard_map/rows_update/pallas_call | solution.py:252
  61.8 0.0 collective-permute-done.1.arrived
  61.8 1.4 %finish.1 = f32[16,64,256]{2,1,0:T(8,128)} custom-call(f32[64,16,256]{2,1,0:T(8,128)S(1)} %get-tuple-element.16.own, bf16[64,16,256]{2,1,0:T(8,128)(2,1)S(1)} %collective-permute-done.1.arrived), custom_call_target="tpu_custom_call" | custom-call | flops 262144 | bytes 3145728 | tf_op jit(solution)/shard_map/finish/pallas_call | solution.py:202
Async XLA Ops:
  0.6 1.9 %copy-start = (s32[2048,64]{0,1:T(8,128)S(1)}, s32[2048,64]{0,1:T(8,128)}, u32[]{:S(2)}) copy-start(s32[2048,64]{0,1:T(8,128)} %param.6) | copy-start | bytes 1572868
  12.6 11.0 %collective-permute-start = (bf16[64,32,256]{2,1,0:T(8,128)(2,1)S(1)}, bf16[64,32,256]{2,1,0:T(8,128)(2,1)S(1)}, u32[]{:S(2)}, u32[]{:S(2)}) collective-permute-start(bf16[64,32,256]{2,1,0:T(8,128)(2,1)S(1)} %get-tuple-element.15), channel_id=1, source_target_pairs={{0,1},{1,0},{2,3},{3,2},{4,5},{5,4},{6,7},{7,6},{8,9},{9,8},{10,11... | collective-permute-start | bytes 3145736 | tf_op jit(solution)/shard_map/ppermute | solution.py:293
  23.8 38.0 %collective-permute-start.1 = (bf16[64,16,256]{2,1,0:T(8,128)(2,1)S(1)}, bf16[64,16,256]{2,1,0:T(8,128)(2,1)S(1)}, u32[]{:S(2)}, u32[]{:S(2)}) collective-permute-start(bf16[64,16,256]{2,1,0:T(8,128)(2,1)S(1)} %get-tuple-element.17), channel_id=1, source_target_pairs={{0,2},{2,0},{1,3},{3,1},{4,6},{6,4},{5,7},{7,5},{8,10},{10,8},{9,1... | collective-permute-start | bytes 1572872 | tf_op jit(solution)/shard_map/ppermute | solution.py:296
  41.3 19.5 %copy-start.1 = (s32[2048]{0:T(1024)S(1)}, s32[2048]{0:T(1024)}, u32[]{:S(2)}) copy-start(s32[2048]{0:T(1024)} %param.7) | copy-start | bytes 24580
  41.4 19.5 %copy-start.2 = (f32[2048]{0:T(1024)S(1)}, f32[2048]{0:T(1024)}, u32[]{:S(2)}) copy-start(f32[2048]{0:T(1024)} %param.8) | copy-start | bytes 24580
  41.4 19.5 %copy-start.3 = (f32[2048]{0:T(1024)S(1)}, f32[2048]{0:T(1024)}, u32[]{:S(2)}) copy-start(f32[2048]{0:T(1024)} %param.9) | copy-start | bytes 24580

commit v4 on v3

--- a/solution.py
+++ b/solution.py
@@ -97,7 +97,7 @@
         for i in range(8)
     ]
     lines.append(jnp.sum(entries, axis=0, keepdims=True))
-    for p in range(32):
+    for p in range(16):
         for i in range(9):
             pay[p, i] = lines[i]
 
@@ -107,7 +107,7 @@
         stage_kernel,
         out_shape=(
             pltpu.VMEM((2 * NODES, ROWS), BF16),
-            pltpu.VMEM((32, 9, 1, 128), F32),
+            pltpu.VMEM((16, 9, 1, 128), F32),
         ),
         in_specs=[VMEM] * 6,
         out_specs=[VMEM] * 2,
@@ -167,25 +167,26 @@
     )(keep, arrived)
 
 
-def relay_kernel(plane, pay):
+def relay_kernel(line, pay):
+    here = lax.axis_index("zl") * 2 + lax.axis_index("core")
     for i in range(9):
-        line = plane[0, i]
-        for p in range(1, 32):
-            line = line + plane[p, i]
-        for p in range(16):
-            pay[p, i] = line
-
-
-def relay(plane):
+        total = line[here, i] if i < 8 else line[0, i]
+        for m in range(1, 4 if i < 8 else 16):
+            total = total + (line[4 * m + here, i] if i < 8 else line[m, i])
+        for p in range(32):
+            pay[p, i] = total
+
+
+def relay(line):
     return pl.pallas_call(
         relay_kernel,
-        out_shape=pltpu.VMEM((16, 9, 1, 128), F32),
+        out_shape=pltpu.VMEM((32, 9, 1, 128), F32),
         in_specs=[VMEM],
         out_specs=VMEM,
         name="relay",
         compiler_params=LIMIT,
         cost_estimate=cost(32 * 9 * 128, 1 << 17),
-    )(plane)
+    )(line)
 
 
 def finish_kernel(own, arrived, histogram, total):
@@ -212,15 +213,14 @@
 
 
 def rows_kernel(parts, node, margin, labels, margin_out, child_out, grad_out, codes_ref):
-    here = lax.axis_index("zl") * 2 + lax.axis_index("core")
     for i in range(8):
-        line = parts[here, i]
-        for z in range(1, 4):
-            line = line + parts[4 * z + here, i]
+        line = parts[0, i]
+        for p in range(1, 32):
+            line = line + parts[p, i]
         codes_ref[i : i + 1, :] = line
     table = parts[0, 8]
-    for m in range(1, 16):
-        table = table + parts[m, 8]
+    for p in range(1, 32):
+        table = table + parts[p, 8]
     codes = codes_ref[...]
     table = jnp.broadcast_to(table, (8, 128))
     rest = pltpu.roll(table, 64, 1) - table
@@ -288,13 +288,13 @@
         far(split_feature.reshape(1, NODES)),
         far(split_bin.reshape(1, NODES)),
     )
-    plane = share(pay, PLANE)
+    line = share(pay, LINE)
     send, keep = histograms(near(weights), columns)
-    arrived = lax.ppermute(send, "core", swap)
-    pay = relay(near(plane))
+    arrived = lax.ppermute(near(send), "core", swap)
+    pay = relay(near(line))
     own, send_line = chip_sum(near(keep), near(arrived))
-    arrived = lax.ppermute(send_line, "zl", swap)
-    parts = share(pay, LINE)
+    arrived = lax.ppermute(near(send_line), "zl", swap)
+    parts = share(pay, PLANE)
     histogram = finish(near(own), near(arrived))
     margin_out, child_out, grad_out = rows_update(
         near(parts),

time: 63.5 us -> 66.2 us (1.043)
  the two profiles are of different devices: /device:TPU:1 before, /device:TPU:8 now
where the time goes in v4:
time: 66.2 us; the launch traced here: 65.9 us
  blocking collectives  41.8 us (63%)
  Pallas kernels  14.6 us (22%)
  starting transfers between devices  6.2 us (9%)
  waiting for transfers between devices  2.63 us (4%)
  between operations  0.71 us (1%)
    all_to_all x2, blocking collectives, share(): return lax.all_to_all(spread, axes, 0, 0, tiled=True)  41.8 us
    pallas_call x1, Pallas kernels, histograms(): pl.pallas_call(histogram_kernel, out_shape=(half, half), in_specs=[VMEM]...  10 us
    ppermute x1, starting transfers between devices, on_device(): arrived = lax.ppermute(near(send_line), 'zl', swap)  4.28 us
    ppermute x1, waiting for transfers between devices, on_device(): arrived = lax.ppermute(near(send), 'core', swap)  2.63 us
    ppermute x1, starting transfers between devices, on_device(): arrived = lax.ppermute(near(send), 'core', swap)  1.92 us
    pallas_call x1, Pallas kernels, stage(): pl.pallas_call(stage_kernel, out_shape=(pltpu.VMEM((2 * NODES, ROWS), BF1...  1.84 us
    pallas_call x1, Pallas kernels, finish(): pl.pallas_call(finish_kernel, out_shape=jax.ShapeDtypeStruct((16, FEATS,...  1.39 us
  transfers between devices with their start and end apart: 2, of which 1 were waited for; matrix products, arithmetic and copies ran while one was open for 0% of the time, Pallas kernels for 2%

profile of v4, /device:TPU:8, one launch (start us, length us, event | category | flops | bytes accessed | tf_op | source)
XLA Modules:
  0.0 65.9 jit_solution(10384651094753929396)
XLA Ops:
  0.6 0.0 copy-start
  0.6 1.8 %stage.1 = (bf16[64,2048]{1,0:T(8,128)(2,1)S(1)}, f32[16,9,1,128]{3,2,1,0:T(1,128)S(1)}) custom-call(s32[64,2048]{1,0:T(8,128)} %bitcast.12, s32[1,2048]{1,0:T(1,128)} %bitcast.14, f32[1,2048]{1,0:T(1,128)} %bitcast.16, f32[1,2048]{1,0:T(1,128)} %bitcast.18, s32[1,32]{1,0:T(1,128)} %bitcast.21, s32[1,32]{1,0:T(1,128)} %bitcast.22), custom_call_target="tpu_custom_call" | custom-call | flops 25165824 | bytes 3145728 | tf_op jit(solution)/shard_map/stage/pallas_call | solution.py:106
  2.5 0.0 copy-done
  2.5 10.0 %histograms.1 = (bf16[64,32,256]{2,1,0:T(8,128)(2,1)S(1)}, bf16[64,32,256]{2,1,0:T(8,128)(2,1)S(1)}) custom-call(bf16[64,2048]{1,0:T(8,128)(2,1)S(1)} %get-tuple-element.13.weights, s32[64,2048]{1,0:T(8,128)S(1)} %bitcast.13), custom_call_target="tpu_custom_call" | custom-call | flops 4294967296 | bytes 3145728 | tf_op jit(solution)/shard_map/histograms/pallas_call | solution.py:137
  12.5 1.9 %collective-permute-start = (bf16[64,32,256]{2,1,0:T(8,128)(2,1)S(1)}, bf16[64,32,256]{2,1,0:T(8,128)(2,1)S(1)}, u32[]{:S(2)}, u32[]{:S(2)}) collective-permute-start(bf16[64,32,256]{2,1,0:T(8,128)(2,1)S(1)} %get-tuple-element.15), channel_id=1, source_target_pairs={{0,1},{1,0},{2,3},{3,2},{4,5},{5,4},{6,7},{7,6},{8,9},{9,8},{10,11... | collective-permute-start | bytes 3145736 | tf_op jit(solution)/shard_map/ppermute | solution.py:293
  14.5 2.6 %collective-permute-done.arrived = bf16[64,32,256]{2,1,0:T(8,128)(2,1)S(1)} collective-permute-done((bf16[64,32,256]{2,1,0:T(8,128)(2,1)S(1)}, bf16[64,32,256]{2,1,0:T(8,128)(2,1)S(1)}, u32[]{:S(2)}, u32[]{:S(2)}) %collective-permute-start) | collective-permute-done | bytes 1048608 | tf_op jit(solution)/shard_map/ppermute | solution.py:293
  17.1 0.2 chip_sum.1
  17.3 4.3 %collective-permute-start.1 = (bf16[64,16,256]{2,1,0:T(8,128)(2,1)S(1)}, bf16[64,16,256]{2,1,0:T(8,128)(2,1)S(1)}, u32[]{:S(2)}, u32[]{:S(2)}) collective-permute-start(bf16[64,16,256]{2,1,0:T(8,128)(2,1)S(1)} %get-tuple-element.17), channel_id=1, source_target_pairs={{0,2},{2,0},{1,3},{3,1},{4,6},{6,4},{5,7},{7,5},{8,10},{10,8},{9,1... | collective-permute-start | bytes 1572872 | tf_op jit(solution)/shard_map/ppermute | solution.py:296
  21.6 21.5 %all_to_all.10.line = f32[16,9,1,128]{3,2,1,0:T(1,128)S(1)} all-to-all(f32[16,9,1,128]{3,2,1,0:T(1,128)S(1)} %get-tuple-element.18), channel_id=1, replica_groups=mesh['x'=4,'y'=8,'zh'=4,'zl'=2,'core'=2] {'zh','zl','core'}, dimensions={0} | all-to-all | bytes 147456 | tf_op jit(solution)/shard_map/all_to_all | solution.py:269
  43.1 0.1 relay.1
  43.2 0.0 copy-start.1
  43.2 0.0 copy-start.2
  43.2 0.0 copy-start.3
  43.2 20.3 %all_to_all.11.parts = f32[32,9,1,128]{3,2,1,0:T(1,128)S(1)} all-to-all(f32[32,9,1,128]{3,2,1,0:T(1,128)S(1)} %relay.1), channel_id=1, replica_groups=mesh['x'=4,'y'=8,'zh'=4,'zl'=2,'core'=2] {'x','y'}, dimensions={0} | all-to-all | bytes 294912 | tf_op jit(solution)/shard_map/all_to_all | solution.py:269
  63.5 0.0 copy-done.1
  63.5 0.0 copy-done.2
  63.5 0.0 copy-done.3
  63.5 1.0 %rows_update.1 = (f32[16,128]{1,0:T(8,128)}, s32[16,128]{1,0:T(8,128)}, f32[2,2048]{1,0:T(2,128)}) custom-call(f32[32,9,1,128]{3,2,1,0:T(1,128)S(1)} %all_to_all.11.parts, s32[16,128]{1,0:T(8,128)S(1)} %bitcast.15, f32[16,128]{1,0:T(8,128)S(1)} %bitcast.17, f32[16,128]{1,0:T(8,128)S(1)} %bitcast.19), custom_call_target="tpu_custom_call" | custom-call | flops 262144 | bytes 131072 | tf_op jit(solution)/shard_map/rows_update/pallas_call | solution.py:252
  64.5 0.0 collective-permute-done.1.arrived
  64.5 1.4 %finish.1 = f32[16,64,256]{2,1,0:T(8,128)} custom-call(f32[64,16,256]{2,1,0:T(8,128)S(1)} %get-tuple-element.16.own, bf16[64,16,256]{2,1,0:T(8,128)(2,1)S(1)} %collective-permute-done.1.arrived), custom_call_target="tpu_custom_call" | custom-call | flops 262144 | bytes 3145728 | tf_op jit(solution)/shard_map/finish/pallas_call | solution.py:203
Async XLA Ops:
  0.6 1.9 %copy-start = (s32[2048,64]{0,1:T(8,128)S(1)}, s32[2048,64]{0,1:T(8,128)}, u32[]{:S(2)}) copy-start(s32[2048,64]{0,1:T(8,128)} %param.6) | copy-start | bytes 1572868
  12.5 4.6 %collective-permute-start = (bf16[64,32,256]{2,1,0:T(8,128)(2,1)S(1)}, bf16[64,32,256]{2,1,0:T(8,128)(2,1)S(1)}, u32[]{:S(2)}, u32[]{:S(2)}) collective-permute-start(bf16[64,32,256]{2,1,0:T(8,128)(2,1)S(1)} %get-tuple-element.15), channel_id=1, source_target_pairs={{0,1},{1,0},{2,3},{3,2},{4,5},{5,4},{6,7},{7,6},{8,9},{9,8},{10,11... | collective-permute-start | bytes 3145736 | tf_op jit(solution)/shard_map/ppermute | solution.py:293
  17.3 47.2 %collective-permute-start.1 = (bf16[64,16,256]{2,1,0:T(8,128)(2,1)S(1)}, bf16[64,16,256]{2,1,0:T(8,128)(2,1)S(1)}, u32[]{:S(2)}, u32[]{:S(2)}) collective-permute-start(bf16[64,16,256]{2,1,0:T(8,128)(2,1)S(1)} %get-tuple-element.17), channel_id=1, source_target_pairs={{0,2},{2,0},{1,3},{3,1},{4,6},{6,4},{5,7},{7,5},{8,10},{10,8},{9,1... | collective-permute-start | bytes 1572872 | tf_op jit(solution)/shard_map/ppermute | solution.py:296
  43.2 20.4 %copy-start.1 = (s32[2048]{0:T(1024)S(1)}, s32[2048]{0:T(1024)}, u32[]{:S(2)}) copy-start(s32[2048]{0:T(1024)} %param.7) | copy-start | bytes 24580
  43.2 20.4 %copy-start.2 = (f32[2048]{0:T(1024)S(1)}, f32[2048]{0:T(1024)}, u32[]{:S(2)}) copy-start(f32[2048]{0:T(1024)} %param.8) | copy-start | bytes 24580
  43.2 20.4 %copy-start.3 = (f32[2048]{0:T(1024)S(1)}, f32[2048]{0:T(1024)}, u32[]{:S(2)}) copy-start(f32[2048]{0:T(1024)} %param.9) | copy-start | bytes 24580
